TPU v7x, 512 devices: a whole 4x8x8 slice. The times are simulated.
512 devices in a mesh: seq: 64 (over z, x, core), head: 8 (over y).
Axes of the slice: x: 4, y: 8, z: 8, core: 2. Of those that a mesh axis runs over, the one named last changes fastest.
Arguments:
- queries: bfloat16 [65536, 3072], P('seq', 'head'), may hold values from -6 to 6
- keys: bfloat16 [65536, 3072], P('seq', 'head'), may hold values from -6 to 6
- values: bfloat16 [65536, 3072], P('seq', 'head'), may hold values from -6 to 6
- tile_pool: int32 [24, 1024], P('head'), may hold values from 0 to 511, as said below
- tile_lists: int32 [24, 512, 12], P('head', 'seq'), may hold values from 0 to 15, as said below
- key_slot: int32 [512], replicated, may hold values from 0 to 511, as said below
Outputs:
- attended: bfloat16 [65536, 3072], P(('seq', 'head'))
Inputs may be any that keep to these rules, and one draw needn't show every extreme that they name: `tile_pool`: for each index i of seq and each group of 3 heads (heads g * 3 onward), the pool entries of those heads for index i (columns i * 16 onward) name tiles whose slots lie on any one index of seq (slot // 8) at most 1 times, and exactly 1 times on some index. `tile_lists`: the 12 entries of one head and one query tile are distinct. `key_slot`: A permutation of the tiles that keeps tiles 0 to 3 at their own slots.
All inputs are finite; a program needn't handle non-finite values.
Results may differ from a plain program's by a relative error of at most 0.0043.
Values may be sent and summed in bfloat16 or wider, within the bound.
A program may use at most 64 MiB of HBM per device.

v0:
```python
import jax
import jax.numpy as jnp
from jax import lax
from jax.sharding import PartitionSpec as P

TILE = 128
SHARED = 4


def from_root(value, axis, source):
    kept = jnp.where(lax.axis_index(axis) == source, value, 0).astype(value.dtype)
    return lax.psum(kept, axis)


def arrange(matrix, tile_count, head_count, head_size):
    return matrix.reshape(tile_count, TILE, head_count, head_size).transpose(2, 0, 1, 3)


def finish(scores, value_part, pattern):
    tile_top = jnp.max(scores, -1)
    weights = jnp.exp(scores - tile_top[..., None])
    row_total = jnp.sum(weights, -1)
    numerator = jnp.einsum(
        pattern, weights.astype(jnp.bfloat16), value_part, preferred_element_type=jnp.float32
    )
    return (numerator, tile_top, row_total)


def blend_tiles(numerator, tile_top, row_total):
    overall = jnp.max(tile_top, 1, keepdims=True)
    factor = jnp.exp(tile_top - overall)
    upper = jnp.sum(factor[..., None] * numerator, 1)
    lower = jnp.sum(factor * row_total, 1)
    return (upper / lower[..., None]).astype(jnp.bfloat16)


def body(queries, keys, values, tile_pool, tile_lists, key_slot):
    seq_count = lax.axis_size("seq")
    my_index = lax.axis_index("seq")
    head_count, pool_total = tile_pool.shape
    pool_len = pool_total // seq_count
    list_len = tile_lists.shape[2]
    rows, width = queries.shape
    head_size = width // head_count
    tile_count = rows // TILE
    bound_slots = (head_count * pool_len + seq_count - 1) // seq_count
    block_tiles = min(tile_count, max(1, 512 // TILE))
    block_count = tile_count // block_tiles
    scaling = head_size ** (-0.5)
    query_heads = arrange(queries, tile_count, head_count, head_size)
    key_value = jnp.concatenate(
        [
            arrange(keys, tile_count, head_count, head_size),
            arrange(values, tile_count, head_count, head_size),
        ],
        -1,
    )
    flat_kv = key_value.reshape(head_count * tile_count, TILE, 2 * head_size)
    shared = from_root(key_value[:, :SHARED], "seq", 0)
    own_pool = lax.dynamic_slice_in_dim(tile_pool, my_index * pool_len, pool_len, 1)
    storage = key_slot[own_pool]
    owner_dev = (storage // tile_count).reshape(-1)
    head_ids = jnp.arange(head_count, dtype=jnp.int32)[:, None]
    req_code = (head_ids * tile_count + storage % tile_count).reshape(-1)
    matches = (owner_dev[:, None] == jnp.arange(seq_count, dtype=jnp.int32)[None, :]).astype(
        jnp.int32
    )
    slot_pos = jnp.sum((jnp.cumsum(matches, 0) - matches) * matches, 1)
    owner_dev, slot_pos, req_code = (owner_dev, slot_pos, req_code)
    outgoing = jnp.zeros((seq_count, bound_slots), jnp.int32).at[owner_dev, slot_pos].set(req_code)
    incoming = lax.all_to_all(outgoing, "seq", split_axis=0, concat_axis=0, tiled=True)
    replies = lax.all_to_all(flat_kv[incoming], "seq", split_axis=0, concat_axis=0, tiled=True)
    pool_tiles = replies[
        owner_dev.reshape(head_count, pool_len), slot_pos.reshape(head_count, pool_len)
    ]
    query_blocks = query_heads.reshape(head_count * block_count, block_tiles, TILE, head_size)
    list_blocks = tile_lists.reshape(head_count * block_count, block_tiles, list_len)
    head_of = jnp.arange(head_count * block_count, dtype=jnp.int32) // block_count

    def per_block(member):
        query_blk, list_blk, head_id = member
        listed = pool_tiles[head_id][list_blk]
        shared_head = shared[head_id]
        common = jnp.broadcast_to(shared_head[None], (block_tiles,) + shared_head.shape)
        keyset = jnp.concatenate([common, listed], 1)
        scores = (
            jnp.einsum(
                "tqd,tjkd->tjqk",
                query_blk,
                keyset[..., :head_size],
                preferred_element_type=jnp.float32,
            )
            * scaling
        )
        numerator, tile_top, row_total = finish(scores, keyset[..., head_size:], "tjqk,tjkd->tjqd")
        return blend_tiles(numerator, tile_top, row_total)

    per_blocks = lax.map(per_block, (query_blocks, list_blocks, head_of))
    per_heads = per_blocks.reshape(head_count, tile_count, TILE, head_size)
    result = per_heads.transpose(1, 2, 0, 3).reshape(rows, width)
    return lax.all_to_all(result, "head", split_axis=0, concat_axis=1, tiled=True)


def solution(mesh):
    return jax.shard_map(
        body,
        mesh=mesh,
        in_specs=(
            P("seq", "head"),
            P("seq", "head"),
            P("seq", "head"),
            P("head", None),
            P("head", "seq", None),
            P(),
        ),
        out_specs=P(("seq", "head"), None),
        check_vma=False,
    )
```

profile of v0, /device:TPU:2, one launch (start us, length us, event | category | flops | bytes accessed | tf_op | source)
XLA Modules:
  0.0 390.8 jit_solution(4417109201509644880)
XLA Ops:
  10.2 13.9 %all-to-all-start = ((s32[64,1,1]{2,1,0:T(1,128)}), s32[64,1,1]{2,1,0:T(1,128)S(1)}, u32[]{:S(2)}, u32[]{:S(2)}) async-start(s32[64,1,1]{2,1,0:T(1,128)} %copy.50), calls=%async_computation | async-start | bytes 65536 | tf_op jit(solution)/shard_map/all_to_all | solution.py:71
  27.5 2.2 copy.49
  29.7 3.0 all-to-all-done
  33.9 2.8 gather_fusion.2
  36.7 7.7 %all-to-all-start.1 = ((bf16[64,1,128,256]{3,2,1,0:T(8,128)(2,1)}), bf16[64,1,128,256]{3,2,1,0:T(8,128)(2,1)}, u32[]{:S(2)}, u32[]{:S(2)}) async-start(bf16[64,1,128,256]{3,2,1,0:T(8,128)(2,1)} %bitcast.115), calls=%async_computation.1 | async-start | bytes 8388608 | tf_op jit(solution)/shard_map/all_to_all | solution.py:72
  47.0 96.1 %all-to-all-done.1 = bf16[64,1,128,256]{3,2,1,0:T(8,128)(2,1)} async-done(((bf16[64,1,128,256]{3,2,1,0:T(8,128)(2,1)}), bf16[64,1,128,256]{3,2,1,0:T(8,128)(2,1)}, u32[]{:S(2)}, u32[]{:S(2)}) %all-to-all-start.1) | async-done | bytes 4194336 | tf_op jit(solution)/shard_map/all_to_all | solution.py:72
  143.1 4.7 %gather_fusion.3 = bf16[48,128,256]{2,1,0:T(8,128)(2,1)} fusion(bf16[64,1,128,256]{3,2,1,0:T(8,128)(2,1)} %all-to-all-done.1, s32[48]{0:T(128)S(1)} %reshape.314), kind=kCustom, calls=%fused_computation.3 | custom fusion | bytes 6291840 | tf_op jit(solution)/shard_map/gather | solution.py:73
  147.8 115.8 %all-reduce.2.cloned.1.call-done = bf16[3,4,128,256]{2,1,3,0:T(4,128)(2,1)} async-done(((bf16[3,4,128,256]{2,1,3,0:T(4,128)(2,1)}), bf16[3,4,128,256]{2,1,3,0:T(4,128)(2,1)}) %all-reduce.2.cloned.1.call-update) | async-done | bytes 786448 | tf_op jit(solution)/shard_map/psum | solution.py:12
  263.6 89.6 %while.10 = (s32[]{:T(128)}, bf16[6,4,128,128]{3,2,1,0:T(8,128)(2,1)S(1)}, s32[6]{0:T(128)S(1)}, bf16[3,4,128,256]{2,1,3,0:T(4,128)(2,1)}, bf16[3,16,128,256]{3,...) while((s32[]{:T(128)}, ...), condition=%wide.region_10.11_spmd, body=%wide.region_4.10_spmd.sunk | while | flops 553721984 | bytes 45364548 | solution.py:98
  268.2 2.5 gather_fusion
  276.1 2.2 multiply_reduce_fusion.5
  283.1 2.5 gather_fusion
  287.0 2.1 bitcast_reduce_fusion.3
  291.0 2.2 multiply_reduce_fusion.5
  298.1 2.5 gather_fusion
  306.0 2.2 multiply_reduce_fusion.5
  313.0 2.5 gather_fusion
  316.9 2.1 bitcast_reduce_fusion.3
  320.9 2.2 multiply_reduce_fusion.5
  328.0 2.5 gather_fusion
  335.9 2.2 multiply_reduce_fusion.5
  342.9 2.5 gather_fusion
  350.8 2.2 multiply_reduce_fusion.5
  354.0 28.4 %all_to_all.33 = bf16[8,128,384]{2,1,0:T(8,128)(2,1)S(1)} all-to-all(bf16[8,128,384]{2,1,0:T(8,128)(2,1)S(1)} %copy.56), channel_id=1, replica_groups=mesh['seq'=64,'head'=8] {'head'}, dimensions={0} | all-to-all | bytes 1572864 | tf_op jit(solution)/shard_map/all_to_all | solution.py:101
  (125 shorter events, 58.0 us)
Async XLA Ops:
  6.5 1.1 copy-start
  6.5 19.2 %copy-start.2 = (bf16[1024,384]{1,0:T(8,128)(2,1)S(1)}, bf16[1024,384]{1,0:T(8,128)(2,1)}, u32[]{:S(2)}) copy-start(bf16[1024,384]{1,0:T(8,128)(2,1)} %param.10) | copy-start | bytes 2359300
  10.2 22.4 %all-to-all-start = ((s32[64,1,1]{2,1,0:T(1,128)}), s32[64,1,1]{2,1,0:T(1,128)S(1)}, u32[]{:S(2)}, u32[]{:S(2)}) async-start(s32[64,1,1]{2,1,0:T(1,128)} %copy.50), calls=%async_computation | async-start | bytes 65536 | tf_op jit(solution)/shard_map/all_to_all | solution.py:71
  36.7 9.3 %copy-start.3 = (bf16[1024,384]{1,0:T(8,128)(2,1)S(1)}, bf16[1024,384]{1,0:T(8,128)(2,1)}, u32[]{:S(2)}) copy-start(bf16[1024,384]{1,0:T(8,128)(2,1)} %param.8) | copy-start | bytes 2359300
  36.7 106.4 %all-to-all-start.1 = ((bf16[64,1,128,256]{3,2,1,0:T(8,128)(2,1)}), bf16[64,1,128,256]{3,2,1,0:T(8,128)(2,1)}, u32[]{:S(2)}, u32[]{:S(2)}) async-start(bf16[64,1,128,256]{3,2,1,0:T(8,128)(2,1)} %bitcast.115), calls=%async_computation.1 | async-start | bytes 8388608 | tf_op jit(solution)/shard_map/all_to_all | solution.py:72
  44.3 219.3 %all-reduce.2.cloned.1.call-start = ((), (), s32[]{:S(2)}) async-start(), calls=%async_computation.3 | async-start | bytes 1572864 | tf_op jit(solution)/shard_map/psum | solution.py:12
  274.2 1.9 copy-start.1
  289.1 1.9 copy-start.1
  304.1 1.9 copy-start.1
  319.0 1.9 copy-start.1
  334.0 1.9 copy-start.1
  348.9 1.9 copy-start.1
Sparse Core Ops, SparseCore 0:
  48.6 214.9 all-reduce.1
where the time goes:
time: 392 us; the launch traced here: 391 us
  waiting for transfers between devices  215 us (55%)
  local copies, waits for them, and re-layouts  55.9 us (14%)
  blocking collectives  28.4 us (7%)
  matrix products  26.3 us (7%)
  starting transfers between devices  21.6 us (6%)
  other arithmetic  18.2 us (5%)
  between operations  13.6 us (3%)
  loops' own time  12.1 us (3%)
    psum x1, waiting for transfers between devices, from_root(): return lax.psum(kept, axis)  116 us
    all_to_all x1, waiting for transfers between devices, body(): lax.all_to_all(flat_kv[incoming], 'seq', split_axis=0, concat_axis=0, til...  96.1 us
    all_to_all x1, blocking collectives, body(): lax.all_to_all(result, 'head', split_axis=0, concat_axis=1, tiled=True)  28.4 us
    gather x6, local copies, waits for them, and re-layouts, per_block(): listed = pool_tiles[head_id][list_blk]  15.1 us
    all_to_all x1, starting transfers between devices, body(): lax.all_to_all(outgoing, 'seq', split_axis=0, concat_axis=0, tiled=True)  13.9 us
    dot_general x6, matrix products, finish(): jnp.einsum(pattern, weights.astype(jnp.bfloat16), value_part, preferred_e...  13.4 us
    dot_general x6, matrix products, per_block(): jnp.einsum('tqd,tjkd->tjqk', query_blk, keyset[..., :head_size], preferre...  12.9 us
    another operation x1, loops' own time, body(): per_blocks = lax.map(per_block, (query_blocks, list_blocks, head_of))  12.1 us
  transfers between devices with their start and end apart: 3, of which 3 were waited for; matrix products, arithmetic and copies ran while one was open for 3% of the time, Pallas kernels for 0%

commit v1 on v0

--- a/solution.py
+++ b/solution.py
@@ -9,7 +9,10 @@
 
 def from_root(value, axis, source):
     kept = jnp.where(lax.axis_index(axis) == source, value, 0).astype(value.dtype)
-    return lax.psum(kept, axis)
+    keep_up_series_all_all = lambda own_rows, chip_axis: jnp.sum(
+        jax.lax.all_gather(own_rows, chip_axis), 0
+    )
+    return keep_up_series_all_all(kept, axis)
 
 
 def arrange(matrix, tile_count, head_count, head_size):

time: 392 us -> 421 us (1.074)
  the two profiles are of different devices: /device:TPU:2 before, /device:TPU:1 now
where the time goes in v1:
time: 421 us; the launch traced here: 420 us
  waiting for transfers between devices  232 us (55%)
  local copies, waits for them, and re-layouts  51.7 us (12%)
  other arithmetic  36.2 us (9%)
  blocking collectives  29.4 us (7%)
  matrix products  26.3 us (6%)
  starting transfers between devices  20.7 us (5%)
  between operations  13.6 us (3%)
  loops' own time  10.1 us (2%)
    all_to_all x1, waiting for transfers between devices, body(): lax.all_to_all(flat_kv[incoming], 'seq', split_axis=0, concat_axis=0, til...  121 us
    all_gather x1, waiting for transfers between devices, from_root(): jax.lax.all_gather(own_rows, chip_axis)  103 us
    all_to_all x1, blocking collectives, body(): lax.all_to_all(result, 'head', split_axis=0, concat_axis=1, tiled=True)  29.4 us
    reduce_sum x1, other arithmetic, from_root(): jnp.sum(jax.lax.all_gather(own_rows, chip_axis), 0)  16.2 us
    gather x6, local copies, waits for them, and re-layouts, per_block(): listed = pool_tiles[head_id][list_blk]  15.1 us
    all_to_all x1, starting transfers between devices, body(): lax.all_to_all(outgoing, 'seq', split_axis=0, concat_axis=0, tiled=True)  14.8 us
    dot_general x6, matrix products, finish(): jnp.einsum(pattern, weights.astype(jnp.bfloat16), value_part, preferred_e...  13.5 us
    dot_general x6, matrix products, per_block(): jnp.einsum('tqd,tjkd->tjqk', query_blk, keyset[..., :head_size], preferre...  12.8 us
  transfers between devices with their start and end apart: 3, of which 3 were waited for; matrix products, arithmetic and copies ran while one was open for 4% of the time, Pallas kernels for 0%

profile of v1, /device:TPU:1, one launch (start us, length us, event | category | flops | bytes accessed | tf_op | source)
XLA Modules:
  0.0 420.0 jit_solution(99563513658989438)
XLA Ops:
  14.9 14.8 %all-to-all-start = ((s32[64,1,1]{2,1,0:T(1,128)}), s32[64,1,1]{2,1,0:T(1,128)S(1)}, u32[]{:S(2)}, u32[]{:S(2)}) async-start(s32[64,1,1]{2,1,0:T(1,128)} %copy.52), calls=%async_computation | async-start | bytes 65536 | tf_op jit(solution)/shard_map/all_to_all | solution.py:74
  31.1 8.0 %all-to-all-done = s32[64,1,1]{2,1,0:T(1,128)S(1)} async-done(((s32[64,1,1]{2,1,0:T(1,128)}), s32[64,1,1]{2,1,0:T(1,128)S(1)}, u32[]{:S(2)}, u32[]{:S(2)}) %all-to-all-start) | async-done | bytes 288 | tf_op jit(solution)/shard_map/all_to_all | solution.py:74
  40.3 2.8 gather_fusion.2
  43.1 5.8 %all-to-all-start.1 = ((bf16[64,1,128,256]{3,2,1,0:T(8,128)(2,1)}), bf16[64,1,128,256]{3,2,1,0:T(8,128)(2,1)}, u32[]{:S(2)}, u32[]{:S(2)}) async-start(bf16[64,1,128,256]{3,2,1,0:T(8,128)(2,1)} %bitcast.117), calls=%async_computation.1 | async-start | bytes 8388608 | tf_op jit(solution)/shard_map/all_to_all | solution.py:75
  51.1 120.9 %all-to-all-done.1 = bf16[64,1,128,256]{3,2,1,0:T(8,128)(2,1)} async-done(((bf16[64,1,128,256]{3,2,1,0:T(8,128)(2,1)}), bf16[64,1,128,256]{3,2,1,0:T(8,128)(2,1)}, u32[]{:S(2)}, u32[]{:S(2)}) %all-to-all-start.1) | async-done | bytes 4194336 | tf_op jit(solution)/shard_map/all_to_all | solution.py:75
  172.0 4.8 %gather_fusion.3 = bf16[48,128,256]{2,1,0:T(8,128)(2,1)} fusion(bf16[64,1,128,256]{3,2,1,0:T(8,128)(2,1)} %all-to-all-done.1, s32[48]{0:T(128)S(1)} %reshape.314), kind=kCustom, calls=%fused_computation.3 | custom fusion | bytes 6291840 | tf_op jit(solution)/shard_map/gather | solution.py:76
  176.7 103.0 %all-gather.3.cloned.1.call-done = bf16[192,4,128,256]{3,2,1,0:T(8,128)(2,1)} async-done(((bf16[3,4,128,256]{3,2,1,0:T(8,128)(2,1)}), bf16[192,4,128,256]{3,2,1,0:T(8,128)(2,1)}) %all-gather.3.cloned.1.call-update) | async-done | bytes 50331664 | tf_op jit(solution)/shard_map/all_gather | solution.py:13
  279.8 16.2 %reduce_sum.52 = bf16[3,4,128,256]{3,2,1,0:T(8,128)(2,1)S(1)} reduce(bf16[64,3,4,128,256]{4,3,2,1,0:T(8,128)(2,1)} %bitcast.114, bf16[]{:T(256)} %constant.84.clone.1), dimensions={0}, to_apply=%region_3.4 | reduce | flops 24772608 | bytes 51118080 | tf_op jit(solution)/shard_map/reduce_sum | solution.py:12
  296.0 84.2 %while.10 = (s32[]{:T(128)}, bf16[6,4,128,128]{3,2,1,0:T(8,128)(2,1)}, s32[6]{0:T(128)S(1)}, bf16[3,4,128,256]{3,2,1,0:T(8,128)(2,1)S(1)}, bf16[3,16,128,256]{3,...) while((s32[]{:T(128)}, ...), condition=%wide.region_10.11_spmd, body=%wide.region_4.10_spmd.sunk | while | flops 553721984 | bytes 44840268 | solution.py:101
  300.4 2.5 gather_fusion
  303.0 2.1 bitcast_reduce_fusion.3
  307.0 2.3 multiply_reduce_fusion.5
  314.5 2.5 gather_fusion
  321.0 2.3 multiply_reduce_fusion.5
  328.5 2.5 gather_fusion
  335.1 2.3 multiply_reduce_fusion.5
  342.5 2.5 gather_fusion
  345.1 2.1 bitcast_reduce_fusion.3
  349.1 2.3 multiply_reduce_fusion.5
  356.6 2.5 gather_fusion
  363.1 2.3 multiply_reduce_fusion.5
  370.6 2.5 gather_fusion
  377.2 2.3 multiply_reduce_fusion.5
  382.1 29.4 %all_to_all.33 = bf16[8,128,384]{2,1,0:T(8,128)(2,1)S(1)} all-to-all(bf16[8,128,384]{2,1,0:T(8,128)(2,1)S(1)} %copy.57), channel_id=1, replica_groups=mesh['seq'=64,'head'=8] {'head'}, dimensions={0} | all-to-all | bytes 1572864 | tf_op jit(solution)/shard_map/all_to_all | solution.py:104
  (121 shorter events, 57.6 us)
Async XLA Ops:
  6.5 5.8 %copy-start = (s32[512]{0:T(512)S(1)}, s32[512]{0:T(512)}, u32[]{:S(2)}) copy-start(s32[512]{0:T(512)} %param.13) | copy-start | bytes 6148
  6.5 273.2 %all-gather.3.cloned.1.call-start = ((), (), s32[]{:S(2)}) async-start(), calls=%async_computation.3 | async-start | bytes 51118080 | tf_op jit(solution)/shard_map/all_gather | solution.py:13
  14.9 24.2 %all-to-all-start = ((s32[64,1,1]{2,1,0:T(1,128)}), s32[64,1,1]{2,1,0:T(1,128)S(1)}, u32[]{:S(2)}, u32[]{:S(2)}) async-start(s32[64,1,1]{2,1,0:T(1,128)} %copy.52), calls=%async_computation | async-start | bytes 65536 | tf_op jit(solution)/shard_map/all_to_all | solution.py:74
  43.1 6.1 %copy-start.3 = (bf16[1024,384]{1,0:T(8,128)(2,1)S(1)}, bf16[1024,384]{1,0:T(8,128)(2,1)}, u32[]{:S(2)}) copy-start(bf16[1024,384]{1,0:T(8,128)(2,1)} %param.8) | copy-start | bytes 2359300
  43.1 128.9 %all-to-all-start.1 = ((bf16[64,1,128,256]{3,2,1,0:T(8,128)(2,1)}), bf16[64,1,128,256]{3,2,1,0:T(8,128)(2,1)}, u32[]{:S(2)}, u32[]{:S(2)}) async-start(bf16[64,1,128,256]{3,2,1,0:T(8,128)(2,1)} %bitcast.117), calls=%async_computation.1 | async-start | bytes 8388608 | tf_op jit(solution)/shard_map/all_to_all | solution.py:75
  305.1 1.9 copy-start.2
  319.1 1.9 copy-start.2
  333.2 1.9 copy-start.2
  347.2 1.9 copy-start.2
  361.2 1.9 copy-start.2
  375.3 1.9 copy-start.2
  380.2 32.9 %copy-start.1 = (s32[512]{0:T(512)S(1)}, s32[512]{0:T(512)}, u32[]{:S(2)}) copy-start(s32[512]{0:T(512)} %param.13) | copy-start | bytes 6148
Sparse Core Ops, SparseCore 0:
  11.4 268.2 all-gather.2
